TPU v7x, 32 devices: a whole 2x2x4 slice. The times are simulated.
32 devices in a mesh: dp: 4 (over x, core), row: 4 (over z), col: 2 (over y).
Axes of the slice: x: 2, y: 2, z: 4, core: 2. Of those that a mesh axis runs over, the one named last changes fastest.
Arguments:
- block_input: bfloat16 [7168, 2048], P(('dp', 'col'), 'row'), may hold values from -6 to 6
- segment_ids: int32 [7168], P(('dp', 'row')), may hold values from 0 to 111, never falling along the last dimension, each value on 1 to 448 neighbouring positions
- attn_gain: float32 [2048], P('row'), may hold values from 0.25 to 1.75
- mix_weight: bfloat16 [2048, 12288], P('row', 'col'), may hold values from -0.125 to 0.125
- decay_weight: bfloat16 [2048, 32], P('row', 'col'), may hold values from -0.125 to 0.125
- conv_weight: float32 [4, 8192], P(None, 'col'), may hold values from -2.5 to 2.5
- decay_log: float32 [16], P('col'), may hold values from -6.5 to -2.5
- decay_bias: float32 [16], P('col'), may hold values from -1.5 to 1
- out_gain: float32 [256], replicated, may hold values from 0.25 to 1.75
- out_weight: bfloat16 [4096, 2048], P('col', 'row'), may hold values from -0.1875 to 0.1875
- ffn_gain: float32 [2048], P('row'), may hold values from 0.25 to 1.75
- gate_weight: bfloat16 [2048, 5632], P('row', 'col'), may hold values from -0.125 to 0.125
- up_weight: bfloat16 [2048, 5632], P('row', 'col'), may hold values from -0.125 to 0.125
- down_weight: bfloat16 [5632, 2048], P('col', 'row'), may hold values from -0.15625 to 0.15625
- cotangent: bfloat16 [7168, 2048], P(('dp', 'col'), 'row'), may hold values from -6 to 6
Outputs:
- block_output: bfloat16 [7168, 2048], P(('dp', 'col'), 'row')
- input_grad: bfloat16 [7168, 2048], P(('dp', 'col'), 'row')
- attn_gain_grad: float32 [2048], P('row')
- mix_weight_grad: float32 [2048, 12288], P('row', 'col')
- decay_weight_grad: float32 [2048, 32], P('row', 'col')
- conv_weight_grad: float32 [4, 8192], P(None, 'col')
- decay_log_grad: float32 [16], P('col')
- decay_bias_grad: float32 [16], P('col')
- out_gain_grad: float32 [256], replicated
- out_weight_grad: float32 [4096, 2048], P('col', 'row')
- ffn_gain_grad: float32 [2048], P('row')
- gate_weight_grad: float32 [2048, 5632], P('row', 'col')
- up_weight_grad: float32 [2048, 5632], P('row', 'col')
- down_weight_grad: float32 [5632, 2048], P('col', 'row')
Inputs may be any that keep to these rules, and one draw needn't show every extreme that they name: `segment_ids`: segment numbers never fall along the tokens; each document has 1 to 448 tokens and one has exactly 448.
All inputs are finite; a program needn't handle non-finite values.
Results may differ from a plain program's by a relative error of at most 0.025.
Values may be sent and summed in bfloat16 or wider, within the bound.
A program may use at most 320 MiB of HBM per device.

v0:
```python
import jax
import jax.numpy as jnp
from jax import lax
from jax.sharding import PartitionSpec as P

D = 2048
BLOCK = 64
SEQ = 448


def block_step(state, inputs):
    query, key, value, beta, decay, starts = inputs
    highest = lax.Precision.HIGHEST
    total = jnp.cumsum(decay, axis=-1)
    marks = jnp.cumsum(starts, axis=-1)
    position = jnp.arange(BLOCK)
    lower = position[:, None] >= position[None, :]
    strict = (position[:, None] > position[None, :]).astype(key.dtype)
    same = (marks[..., :, None] == marks[..., None, :]) & lower
    spread = total[..., :, None] - total[..., None, :]
    weight = jnp.where(same, jnp.exp(jnp.where(same, spread, 0.0)), 0.0)
    carried = jnp.where(marks == 0.0, jnp.exp(total), 0.0)
    inner = jnp.einsum("chtk,chsk->chts", key, key, precision=highest)
    system = jnp.eye(BLOCK, dtype=key.dtype) + beta[..., None] * weight * strict * inner
    known = jnp.einsum("chtk,chkv->chtv", key, state, precision=highest)
    target = beta[..., None] * (value - carried[..., None] * known)
    fresh = jax.scipy.linalg.solve_triangular(system, target, lower=True, unit_diagonal=True)
    scores = jnp.einsum("chtk,chsk->chts", query, key, precision=highest) * weight
    result = carried[..., None] * jnp.einsum("chtk,chkv->chtv", query, state, precision=highest)
    result = result + jnp.einsum("chts,chsv->chtv", scores, fresh, precision=highest)
    last_row = weight[..., -1, :]
    new_state = carried[..., -1][..., None, None] * state
    new_state = new_state + jnp.einsum(
        "chsk,chsv->chkv", key * last_row[..., None], fresh, precision=highest
    )
    return (new_state, result)


def mix_core(proj, decay_in, conv_w, decay_log, decay_bias, out_gain, segments):
    count, length, width = proj.shape
    heads = decay_log.shape[0]
    value_dim = out_gain.shape[0]
    per_head = width // heads
    key_dim = (per_head - 2 * value_dim) // 2
    inner_width = 2 * key_dim + value_dim
    split = proj.reshape(count, length, heads, per_head)
    conv_in = split[..., :inner_width].reshape(count, length, heads * inner_width)
    gate_out = split[..., inner_width:]
    taps = conv_w.shape[0]
    summed = jnp.zeros_like(conv_in)
    for lag in range(taps):
        moved = jnp.pad(conv_in, ((0, 0), (lag, 0), (0, 0)))[:, :length]
        moved_seg = jnp.pad(segments, ((0, 0), (lag, 0)), constant_values=-1)[:, :length]
        keep = (moved_seg == segments).astype(proj.dtype)[..., None]
        summed = summed + conv_w[taps - 1 - lag] * moved * keep
    active = jax.nn.silu(summed).reshape(count, length, heads, inner_width)
    query = active[..., :key_dim]
    key = active[..., key_dim : 2 * key_dim]
    value = active[..., 2 * key_dim :]
    query = (
        query
        * lax.rsqrt(jnp.sum(query * query, axis=-1, keepdims=True) + 1e-06)
        * key_dim ** (-0.5)
    )
    key = key * lax.rsqrt(jnp.sum(key * key, axis=-1, keepdims=True) + 1e-06)
    paired = decay_in.reshape(count, length, heads, 2)
    beta = jax.nn.sigmoid(paired[..., 0])
    decay = -jnp.exp(decay_log) * jax.nn.softplus(paired[..., 1] + decay_bias)
    prior = jnp.pad(segments, ((0, 0), (1, 0)), constant_values=-1)[:, :length]
    starts = jnp.broadcast_to(
        (prior != segments).astype(proj.dtype)[..., None], (count, length, heads)
    )
    blocks = length // BLOCK

    def to_blocks(values):
        values = values.reshape((count, blocks, BLOCK) + values.shape[2:])
        values = jnp.moveaxis(values, 1, 0)
        return jnp.moveaxis(values, 3, 2)

    inputs = (
        to_blocks(query),
        to_blocks(key),
        to_blocks(value),
        to_blocks(beta),
        to_blocks(decay),
        to_blocks(starts),
    )
    state = jnp.zeros((count, heads, key_dim, value_dim), proj.dtype)
    state, outputs = lax.scan(jax.checkpoint(block_step), state, inputs)
    outputs = jnp.moveaxis(jnp.moveaxis(outputs, 3, 2), 0, 1).reshape(
        count, length, heads, value_dim
    )
    normed = outputs * lax.rsqrt(jnp.mean(outputs * outputs, axis=-1, keepdims=True) + 1e-05)
    normed = normed * out_gain * jax.nn.silu(gate_out)
    return normed.reshape(count, length, heads * value_dim)


def project(left, right):
    return jnp.dot(left, right, preferred_element_type=jnp.float32)


def project_back(left, right):
    return jnp.einsum("tn,kn->tk", left, right, preferred_element_type=jnp.float32)


def weight_grad(left, right):
    return jnp.einsum("tk,tn->kn", left, right, preferred_element_type=jnp.float32)


def norm_forward(values):
    local_sum = jnp.sum(values * values, axis=1)
    total = lax.psum(local_sum, "row")
    scale = lax.rsqrt(total / D + 1e-05)[:, None]
    return (values * scale, scale)


def norm_backward(grad_normed, normed, scale, gain):
    scaled = grad_normed * gain
    local_sum = jnp.sum(scaled * normed, axis=1)
    total = lax.psum(local_sum, "row")
    grad_input = scale * (scaled - normed * (total / D)[:, None])
    return (grad_input, jnp.sum(grad_normed * normed, axis=0))


def gather_tokens(values):
    return lax.all_gather(values, "col", axis=0, tiled=True)


def gather_grads(values):
    return lax.all_gather(values, "col", axis=0, tiled=True)


def split_rows(first, second):
    return (
        lax.psum_scatter(first, "row", scatter_dimension=0, tiled=True),
        lax.psum_scatter(second, "row", scatter_dimension=0, tiled=True),
    )


def join_rows(values):
    return lax.all_gather(values, "row", axis=0, tiled=True)


def join_grads(first, second):
    return (
        lax.all_gather(first, "row", axis=0, tiled=True),
        lax.all_gather(second, "row", axis=0, tiled=True),
    )


def sum_to_tokens(whole, weight, out_rows):

    def term(start, count):
        return project(whole, weight)

    return lax.psum_scatter(
        term(jnp.int32(0), lax.axis_size("col") * out_rows).astype(jnp.bfloat16),
        "col",
        scatter_dimension=0,
        tiled=True,
    ).astype(jnp.float32)


def grads_to_tokens(wholes, weights, out_rows):

    def term(start, count):
        total = project_back(wholes[0], weights[0])
        return total + project_back(wholes[1], weights[1])

    return lax.psum_scatter(
        term(jnp.int32(0), lax.axis_size("col") * out_rows).astype(jnp.bfloat16),
        "col",
        scatter_dimension=0,
        tiled=True,
    ).astype(jnp.float32)


def grads_to_rows(whole, weight, out_rows):

    def term(start, count):
        return project_back(whole, weight)

    return lax.psum_scatter(
        term(jnp.int32(0), lax.axis_size("row") * out_rows).astype(jnp.bfloat16),
        "row",
        scatter_dimension=0,
        tiled=True,
    ).astype(jnp.float32)


def swiglu_back(grad_hidden, gate, up_values):
    sigmoid_gate = jax.nn.sigmoid(gate)
    grad_gate = grad_hidden * up_values * sigmoid_gate * (1.0 + gate * (1.0 - sigmoid_gate))
    grad_up = grad_hidden * gate * sigmoid_gate
    return (grad_gate.astype(jnp.bfloat16), grad_up.astype(jnp.bfloat16))


def on_device(
    block_input,
    segment_ids,
    attn_gain,
    mix_weight,
    decay_weight,
    conv_weight,
    decay_log,
    decay_bias,
    out_gain,
    out_weight,
    ffn_gain,
    gate_weight,
    up_weight,
    down_weight,
    cotangent,
):
    stored = block_input.astype(jnp.float32)
    local_rows = stored.shape[0]
    normed_one, scale_one = norm_forward(stored)
    attn_input = (normed_one * attn_gain).astype(jnp.bfloat16)
    attn_all = gather_tokens(attn_input)
    proj, decay_in = split_rows(project(attn_all, mix_weight), project(attn_all, decay_weight))
    mixer_rows = proj.shape[0]
    sequences = mixer_rows // SEQ
    segments = segment_ids.reshape(sequences, SEQ)

    def mixer(proj_rows, decay_rows, conv_local, log_local, bias_local, gain_local):
        result = mix_core(
            proj_rows.reshape(sequences, SEQ, -1),
            decay_rows.reshape(sequences, SEQ, -1),
            conv_local,
            log_local,
            bias_local,
            gain_local,
            segments,
        )
        return result.reshape(mixer_rows, -1)

    mixed, mixer_back = jax.vjp(mixer, proj, decay_in, conv_weight, decay_log, decay_bias, out_gain)
    mixed_all = join_rows(mixed.astype(jnp.bfloat16))
    residual = stored + sum_to_tokens(mixed_all, out_weight, local_rows)
    normed_two, scale_two = norm_forward(residual)
    ffn_input = (normed_two * ffn_gain).astype(jnp.bfloat16)
    ffn_all = gather_tokens(ffn_input)
    gate, up_values = (
        lax.psum(project(ffn_all, gate_weight).astype(jnp.bfloat16), "row").astype(jnp.float32),
        lax.psum(project(ffn_all, up_weight).astype(jnp.bfloat16), "row").astype(jnp.float32),
    )
    hidden_all = (jax.nn.silu(gate) * up_values).astype(jnp.bfloat16)
    block_output = (residual + sum_to_tokens(hidden_all, down_weight, local_rows)).astype(
        jnp.bfloat16
    )
    out_grads = gather_grads(cotangent)
    down_grad = weight_grad(hidden_all, out_grads)
    grad_hidden = lax.psum(project_back(out_grads, down_weight).astype(jnp.bfloat16), "row").astype(
        jnp.float32
    )
    grad_gate, grad_up = swiglu_back(grad_hidden, gate, up_values)
    gate_grad = weight_grad(ffn_all, grad_gate)
    up_grad = weight_grad(ffn_all, grad_up)
    grad_ffn_in = grads_to_tokens((grad_gate, grad_up), (gate_weight, up_weight), local_rows)
    grad_from_ffn, ffn_gain_part = norm_backward(grad_ffn_in, normed_two, scale_two, ffn_gain)
    grad_residual = cotangent.astype(jnp.float32) + grad_from_ffn
    branch_grads = gather_grads(grad_residual.astype(jnp.bfloat16))
    out_weight_grad = weight_grad(mixed_all, branch_grads)
    grad_mixed = grads_to_rows(branch_grads, out_weight, mixer_rows)
    grad_proj, grad_decay_in, conv_part, log_part, bias_part, gain_part = mixer_back(grad_mixed)
    proj_grads, decay_grads = join_grads(
        grad_proj.astype(jnp.bfloat16), grad_decay_in.astype(jnp.bfloat16)
    )
    mix_grad = weight_grad(attn_all, proj_grads)
    decay_grad = weight_grad(attn_all, decay_grads)
    grad_attn_in = grads_to_tokens(
        (proj_grads, decay_grads), (mix_weight, decay_weight), local_rows
    )
    grad_from_attn, attn_gain_part = norm_backward(grad_attn_in, normed_one, scale_one, attn_gain)
    input_grad = (grad_residual + grad_from_attn).astype(jnp.bfloat16)
    summed = (
        lax.psum(mix_grad.astype(jnp.bfloat16), "dp").astype(jnp.float32),
        lax.psum(decay_grad.astype(jnp.bfloat16), "dp").astype(jnp.float32),
        lax.psum(out_weight_grad.astype(jnp.bfloat16), "dp").astype(jnp.float32),
        lax.psum(gate_grad.astype(jnp.bfloat16), "dp").astype(jnp.float32),
        lax.psum(up_grad.astype(jnp.bfloat16), "dp").astype(jnp.float32),
        lax.psum(down_grad.astype(jnp.bfloat16), "dp").astype(jnp.float32),
    )
    row_index = lax.axis_index("row")
    col_index = lax.axis_index("col")
    row_pick = (jnp.arange(lax.axis_size("row")) == row_index).astype(jnp.float32)
    col_pick = (jnp.arange(lax.axis_size("col")) == col_index).astype(jnp.float32)
    small = lax.psum(
        (
            row_pick[:, None] * attn_gain_part[None, :],
            row_pick[:, None] * ffn_gain_part[None, :],
            col_pick[:, None, None] * conv_part[None],
            col_pick[:, None] * log_part[None, :],
            col_pick[:, None] * bias_part[None, :],
            gain_part,
        ),
        ("dp", "row", "col"),
    )
    attn_gain_grad = lax.dynamic_index_in_dim(small[0], row_index, 0, keepdims=False)
    ffn_gain_grad = lax.dynamic_index_in_dim(small[1], row_index, 0, keepdims=False)
    conv_grad = lax.dynamic_index_in_dim(small[2], col_index, 0, keepdims=False)
    log_grad = lax.dynamic_index_in_dim(small[3], col_index, 0, keepdims=False)
    bias_grad = lax.dynamic_index_in_dim(small[4], col_index, 0, keepdims=False)
    return (
        block_output,
        input_grad,
        attn_gain_grad,
        summed[0],
        summed[1],
        conv_grad,
        log_grad,
        bias_grad,
        small[5],
        summed[2],
        ffn_gain_grad,
        summed[3],
        summed[4],
        summed[5],
    )


def solution(mesh):
    return jax.shard_map(
        on_device,
        mesh=mesh,
        in_specs=(
            P(("dp", "col"), "row"),
            P(("dp", "row")),
            P("row"),
            P("row", "col"),
            P("row", "col"),
            P(None, "col"),
            P("col"),
            P("col"),
            P(),
            P("col", "row"),
            P("row"),
            P("row", "col"),
            P("row", "col"),
            P("col", "row"),
            P(("dp", "col"), "row"),
        ),
        out_specs=(
            P(("dp", "col"), "row"),
            P(("dp", "col"), "row"),
            P("row"),
            P("row", "col"),
            P("row", "col"),
            P(None, "col"),
            P("col"),
            P("col"),
            P(),
            P("col", "row"),
            P("row"),
            P("row", "col"),
            P("row", "col"),
            P("col", "row"),
        ),
        check_vma=False,
    )
```

profile of v0, /device:TPU:0, one launch (start us, length us, event | category | flops | bytes accessed | tf_op | source)
XLA Modules:
  0.0 4328.8 jit_solution(5476020139172058934)
XLA Ops:
  25.4 28.5 all-gather.8.cloned.1.call-done
  56.9 22.5 fusion.207
  84.8 718.7 %reduce-scatter.10.cloned.1.call-done = f32[448,6144]{1,0:T(8,128)} async-done(((f32[1792,6144]{1,0:T(8,128)}), f32[448,6144]{1,0:T(8,128)}) %reduce-scatter.10.cloned.1.call-update) | async-done | bytes 11010064 | tf_op jit(solution)/shard_map/reduce_scatter | solution.py:135
  874.3 405.6 %while.44 = (s32[]{:T(128)}, f32[1,8,128,256]{3,2,1,0:T(8,128)}, f32[7,1,8,64,256]{4,2,3,0,1:T(8,128)}, f32[7,1,8,128,256]{4,3,2,1,0:T(8,128)}, f32[7,1,8,64]{3,...) while((s32[]{:T(128)}, f32[1,8,128,256]{3,2,1,0:T(8,128)}, ...), condition=%wide.region_9.11_spmd.clone.clone, body=%wide.region_6.10_spmd.clone.clone.sunk | while | flops 908922432 | bytes 18620180 | solution.py:89
  877.6 40.0 custom-call.26
  933.9 40.0 custom-call.26
  992.0 40.0 custom-call.26
  1050.2 40.0 custom-call.26
  1108.4 40.0 custom-call.26
  1166.6 40.0 custom-call.26
  1224.7 40.0 custom-call.26
  1288.5 134.2 %all-gather.10.cloned.1.call-done = bf16[1792,2048]{1,0:T(8,128)(2,1)} async-done(((bf16[448,2048]{1,0:T(8,128)(2,1)}), bf16[1792,2048]{1,0:T(8,128)(2,1)}) %all-gather.10.cloned.1.call-update) | async-done | bytes 7340048 | tf_op jit(solution)/shard_map/all_gather | solution.py:141
  1432.3 26.7 reduce-scatter.12.cloned.1.call-done
  1500.6 22.3 all-gather.12.cloned.1.call-done
  1540.9 1000.2 %all-reduce.31.cloned.1.call-done = (bf16[1792,2816]{1,0:T(8,128)(2,1)}, bf16[1792,2816]{1,0:T(8,128)(2,1)}, bf16[1792,2816]{1,0:T(8,128)(2,1)}) async-done(((bf16[1792,2816]{1,0:T(8,128)(2,1)}, bf16[1792,2816]{1,0:T(8,128)(2,1)}, bf16[1792,2816]{1,0:T(8,128)(2,1)}), (bf16[1792,2816]{1,0:T(8,128)(2,1)}, bf16[1792,2816]{1,0:T(8,128)(2,1)}, bf16[1792,2816]{1,0:T(8,128)(2,1)})) %all-reduce.31.cloned.1.call-update) | async-done | bytes 30277648 | tf_op jit(solution)/shard_map/psum | solution.py:245
  2576.8 27.9 reduce-scatter.16.cloned.1.call-done
  2622.3 27.1 all-gather.16.cloned.1.call-done
  2658.7 127.8 %reduce-scatter.18.cloned.1.call-done = bf16[448,2048]{1,0:T(8,128)(2,1)} async-done(((bf16[1792,2048]{1,0:T(8,128)(2,1)}), bf16[448,2048]{1,0:T(8,128)(2,1)}) %reduce-scatter.18.cloned.1.call-update) | async-done | bytes 1835024 | tf_op jit(solution)/shard_map/reduce_scatter | solution.py:183
  2808.8 547.6 %while.43 = (s32[]{:T(128)}, f32[1,8,128,256]{2,3,1,0:T(8,128)}, f32[7,1,8,64,128]{4,2,3,0,1:T(8,128)}, f32[7,1,8,64,128]{4,2,3,0,1:T(8,128)}, f32[7,1,8,64,256]...) while((s32[]{:T(128)}, f32[1,8,128,256]{2,3,1,0:T(8,128)}, ...), condition=%wide.region_35.37_spmd.clone, body=%wide.region_23.36_spmd.clone.sunk | while | flops 2448786944 | bytes 53756548 | solution.py:89
  2819.4 40.7 custom-call.25
  2897.7 40.7 custom-call.25
  2976.0 40.7 custom-call.25
  3054.3 40.7 custom-call.25
  3132.7 40.7 custom-call.25
  3211.0 40.7 custom-call.25
  3289.3 40.7 custom-call.25
  3456.5 356.3 %all-gather.18.cloned.1.call-done = bf16[1792,6144]{1,0:T(8,128)(2,1)} async-done(((bf16[448,6144]{1,0:T(8,128)(2,1)}), bf16[1792,6144]{1,0:T(8,128)(2,1)}) %all-gather.18.cloned.1.call-update) | async-done | bytes 22020112 | tf_op jit(solution)/shard_map/all_gather | solution.py:146
  3812.9 19.4 add_convert_fusion.1
  3909.2 30.7 all-reduce.29.cloned.1.call-done
  3941.3 28.6 reduce-scatter.20.cloned.1.call-done
  3972.0 40.0 all-reduce.22
  4028.7 272.0 %all-reduce.33.cloned.1.call-done = (bf16[512,6144]{1,0:T(8,128)(2,1)}, bf16[2048,512]{1,0:T(8,128)(2,1)}, bf16[512,2816]{1,0:T(8,128)(2,1)}, bf16[512,2816]{1,0:T(8,128)(2,1)}, bf16[2816,512]{1,0:T(8,128)(2,1)}) async-done(((bf16[512,6144]{1,0:T(8,128)(2,1)}, bf16[2048,512]{1,0:T(8,128)(2,1)}, bf16[512,2816]{1,0:T(8,128)(2,1)}, bf16[512,2816]{1,0:T(8,128)(2,1)}, bf16[2816,512]{1,0:T(8,128)(2,1)}), ...) | async-done | bytes 17039376 | tf_op jit(solution)/shard_map/psum | solution.py:277
  (995 shorter events, 862.3 us)
Async XLA Ops:
  7.2 1525.9 %copy-start = (bf16[512,2816]{1,0:T(8,128)(2,1)S(1)}, bf16[512,2816]{1,0:T(8,128)(2,1)}, u32[]{:S(2)}) copy-start(bf16[512,2816]{1,0:T(8,128)(2,1)} %param.32) | copy-start | bytes 8650756
  7.2 46.6 %all-gather.8.cloned.1.call-start = ((), (), s32[]{:S(2)}) async-start(), calls=%async_computation.7 | async-start | bytes 2752512 | tf_op jit(solution)/shard_map/all_gather | solution.py:126
  25.3 56.8 %reduce-scatter.22.cloned.1.call-start = ((), (), s32[]{:S(2)}) async-start(), calls=%async_computation.20 | async-start | bytes 1146880
  56.9 746.6 %reduce-scatter.10.cloned.1.call-start = ((), (), s32[]{:S(2)}) async-start(), calls=%async_computation.8 | async-start | bytes 55050240 | tf_op jit(solution)/shard_map/reduce_scatter | solution.py:135
  79.5 1343.3 %all-gather.10.cloned.1.call-start = ((), (), s32[]{:S(2)}) async-start(), calls=%async_computation.9 | async-start | bytes 9175040 | tf_op jit(solution)/shard_map/all_gather | solution.py:141
  80.3 736.6 %copy-start.71 = (f32[8]{0:T(128)}, f32[8]{0:T(128)S(1)}, u32[]{:S(2)}) copy-start(f32[8]{0:T(128)S(1)} %exponential_negate_fusion) | copy-start | bytes 100
  80.4 752.5 %copy-start.57 = (f32[1,448]{1,0:T(1,128)}, f32[1,448]{1,0:T(1,128)S(1)}, u32[]{:S(2)}) copy-start(f32[1,448]{1,0:T(1,128)S(1)} %get-tuple-element.925) | copy-start | bytes 5380
  80.4 752.5 %copy-start.59 = (f32[1,448]{1,0:T(1,128)}, f32[1,448]{1,0:T(1,128)S(1)}, u32[]{:S(2)}) copy-start(f32[1,448]{1,0:T(1,128)S(1)} %get-tuple-element.926) | copy-start | bytes 5380
  80.4 752.5 %copy-start.61 = (f32[1,448]{1,0:T(1,128)}, f32[1,448]{1,0:T(1,128)S(1)}, u32[]{:S(2)}) copy-start(f32[1,448]{1,0:T(1,128)S(1)} %get-tuple-element.927) | copy-start | bytes 5380
  80.5 752.4 %copy-start.31 = (f32[1,4096]{1,0:T(1,128)}, f32[1,4096]{1,0:T(1,128)S(1)}, u32[]{:S(2)}) copy-start(f32[1,4096]{1,0:T(1,128)S(1)} %get-tuple-element.917) | copy-start | bytes 49156
  80.5 752.4 %copy-start.33 = (f32[1,4096]{1,0:T(1,128)}, f32[1,4096]{1,0:T(1,128)S(1)}, u32[]{:S(2)}) copy-start(f32[1,4096]{1,0:T(1,128)S(1)} %get-tuple-element.918) | copy-start | bytes 49156
  80.5 752.4 %copy-start.35 = (f32[1,4096]{1,0:T(1,128)}, f32[1,4096]{1,0:T(1,128)S(1)}, u32[]{:S(2)}) copy-start(f32[1,4096]{1,0:T(1,128)S(1)} %get-tuple-element.919) | copy-start | bytes 49156
  80.5 752.4 %copy-start.37 = (f32[1,4096]{1,0:T(1,128)}, f32[1,4096]{1,0:T(1,128)S(1)}, u32[]{:S(2)}) copy-start(f32[1,4096]{1,0:T(1,128)S(1)} %get-tuple-element.920) | copy-start | bytes 49156
  83.3 733.6 %copy-start.39 = (f32[1,448,8,1]{1,3,2,0:T(1,128)}, f32[1,448,8,1]{1,3,2,0:T(1,128)S(1)}, u32[]{:S(2)}) copy-start(f32[1,448,8,1]{1,3,2,0:T(1,128)S(1)} %get-tuple-element.921) | copy-start | bytes 43012
  84.0 732.9 %copy-start.29 = (f32[1,7,64,8]{2,1,3,0:T(8,128)}, f32[1,7,64,8]{2,1,3,0:T(8,128)S(1)}, u32[]{:S(2)}) copy-start(f32[1,7,64,8]{2,1,3,0:T(8,128)S(1)} %squeeze.150) | copy-start | bytes 43012
  1288.5 170.5 %reduce-scatter.12.cloned.1.call-start = ((), (), s32[]{:S(2)}) async-start(), calls=%async_computation.10 | async-start | bytes 2752512 | tf_op jit(solution)/shard_map/reduce_scatter | solution.py:156
  1431.6 58.9 %all-gather.14.cloned.1.call-start = ((), (), s32[]{:S(2)}) async-start(), calls=%async_computation.13 | async-start | bytes 2752512 | tf_op jit(solution)/shard_map/all_gather | solution.py:130
  1432.2 90.7 %all-gather.12.cloned.1.call-start = ((), (), s32[]{:S(2)}) async-start(), calls=%async_computation.11 | async-start | bytes 2752512 | tf_op jit(solution)/shard_map/all_gather | solution.py:126
  1472.7 1146.3 %copy-start.48 = (f32[896]{0:T(1024)}, f32[896]{0:T(1024)S(1)}, u32[]{:S(2)}) copy-start(f32[896]{0:T(1024)S(1)} %add_rsqrt_fusion.2) | copy-start | bytes 10756
  1475.4 1065.7 %all-reduce.31.cloned.1.call-start = ((), (), s32[]{:S(2)}) async-start(), calls=%async_computation.21 | async-start | bytes 60555264 | tf_op jit(solution)/shard_map/psum | solution.py:245
  1540.9 1063.8 %reduce-scatter.16.cloned.1.call-start = ((), (), s32[]{:S(2)}) async-start(), calls=%async_computation.14 | async-start | bytes 2752512 | tf_op jit(solution)/shard_map/reduce_scatter | solution.py:170
  2576.8 72.7 %all-gather.16.cloned.1.call-start = ((), (), s32[]{:S(2)}) async-start(), calls=%async_computation.15 | async-start | bytes 2752512 | tf_op jit(solution)/shard_map/all_gather | solution.py:130
  2621.9 164.6 %reduce-scatter.18.cloned.1.call-start = ((), (), s32[]{:S(2)}) async-start(), calls=%async_computation.16 | async-start | bytes 9175040 | tf_op jit(solution)/shard_map/reduce_scatter | solution.py:183
  2658.6 1154.2 %all-gather.18.cloned.1.call-start = ((), (), s32[]{:S(2)}) async-start(), calls=%async_computation.17 | async-start | bytes 27525120 | tf_op jit(solution)/shard_map/all_gather | solution.py:146
  3438.2 501.6 %all-reduce.29.cloned.1.call-start = ((), (), s32[]{:S(2)}) async-start(), calls=%async_computation.19 | async-start | bytes 262144 | tf_op jit(solution)/shard_map/psum | solution.py:288
  3456.5 513.5 %reduce-scatter.20.cloned.1.call-start = ((), (), s32[]{:S(2)}) async-start(), calls=%async_computation.18 | async-start | bytes 2752512 | tf_op jit(solution)/shard_map/reduce_scatter | solution.py:170
  3832.2 192.6 %reduce-scatter.14.cloned.1.call-start = ((), (), s32[]{:S(2)}) async-start(), calls=%async_computation.12 | async-start | bytes 2752512 | tf_op jit(solution)/shard_map/reduce_scatter | solution.py:156
  3842.2 458.5 %all-reduce.33.cloned.1.call-start = ((), (), s32[]{:S(2)}) async-start(), calls=%async_computation.22 | async-start | bytes 34078720 | tf_op jit(solution)/shard_map/psum | solution.py:277
  3895.0 129.9 %copy-start.14 = (bf16[896,512]{1,0:T(8,128)(2,1)S(1)}, bf16[896,512]{1,0:T(8,128)(2,1)}, u32[]{:S(2)}) copy-start(bf16[896,512]{1,0:T(8,128)(2,1)} %reduce-scatter.12.cloned.1.call-done) | copy-start | bytes 2752516
  3895.0 129.9 %copy-start.21 = (bf16[896,512]{1,0:T(8,128)(2,1)S(1)}, bf16[896,512]{1,0:T(8,128)(2,1)}, u32[]{:S(2)}) copy-start(bf16[896,512]{1,0:T(8,128)(2,1)} %param.35) | copy-start | bytes 2752516
  3895.0 129.9 %copy-start.49 = (f32[896]{0:T(1024)S(1)}, f32[896]{0:T(1024)}, u32[]{:S(2)}) copy-start(f32[896]{0:T(1024)} %copy-done.48) | copy-start | bytes 10756
  3895.0 129.9 %copy-start.56 = (f32[896]{0:T(1024)S(1)}, f32[896]{0:T(1024)}, u32[]{:S(2)}) copy-start(f32[896]{0:T(1024)} %copy-done.55) | copy-start | bytes 10756
  (112 other events, 1983.4 us)
Sparse Core Ops, SparseCore 0:
  25.4 28.3 all-gather.7
  57.0 25.0 reduce-scatter.21
  84.5 718.8 reduce-scatter.9
  1288.6 134.0 all-gather.9
  1431.7 27.1 reduce-scatter.11
  1460.4 30.1 all-gather.13
  1492.7 30.1 all-gather.11
  1541.0 1000.0 all-reduce.30
  2576.9 27.7 reduce-scatter.15
  2622.0 27.3 all-gather.15
  2658.7 127.7 reduce-scatter.17
  3438.3 374.4 all-gather.17
  3819.0 120.8 all-reduce.28
  3941.9 27.9 reduce-scatter.19
  3972.1 29.4 reduce-scatter.13
  4005.7 294.9 all-reduce.32
where the time goes:
time: 4340 us; the launch traced here: 4330 us
  waiting for transfers between devices  2820 us (65%)
  other arithmetic  776 us (18%)
  matrix products  417 us (10%)
  local copies, waits for them, and re-layouts  184 us (4%)
  blocking collectives  112 us (3%)
    psum x1, waiting for transfers between devices, on_device(): lax.psum(project(ffn_all, up_weight).astype(jnp.bfloat16), 'row')  1000 us
    reduce_scatter x1, waiting for transfers between devices, split_rows(): lax.psum_scatter(first, 'row', scatter_dimension=0, tiled=True)  719 us
    another operation x56, other arithmetic, block_step(): jax.scipy.linalg.solve_triangular(system, target, lower=True, unit_diagon...  573 us
    all_gather x1, waiting for transfers between devices, join_grads(): lax.all_gather(first, 'row', axis=0, tiled=True)  356 us
    psum x1, waiting for transfers between devices, on_device(): lax.psum(mix_grad.astype(jnp.bfloat16), 'dp').astype(jnp.float32)  272 us
    all_gather x1, waiting for transfers between devices, join_rows(): return lax.all_gather(values, 'row', axis=0, tiled=True)  134 us
    reduce_scatter x1, waiting for transfers between devices, grads_to_rows(): lax.psum_scatter(term(jnp.int32(0), lax.axis_size('row') * out_rows).asty...  128 us
  transfers between devices with their start and end apart: 16, of which 15 were waited for; matrix products, arithmetic and copies ran while one was open for 3% of the time, Pallas kernels for 0%

commit v1 on v0

--- a/solution.py
+++ b/solution.py
@@ -6,6 +6,13 @@
 D = 2048
 BLOCK = 64
 SEQ = 448
+
+
+def face_read(unit, group_axis):
+    by_rank = []
+    for _ in range(lax.psum(1, group_axis)):
+        by_rank.append(unit)
+    return jnp.concatenate(lax.all_to_all(jnp.stack(by_rank), group_axis, 0, 0), axis=0)
 
 
 def block_step(state, inputs):
@@ -138,7 +145,7 @@
 
 
 def join_rows(values):
-    return lax.all_gather(values, "row", axis=0, tiled=True)
+    return face_read(values, "row")
 
 
 def join_grads(first, second):

time: 4340 us -> 4370 us (level)
  blocking collectives: 112 us -> 278 us
  waiting for transfers between devices: 2820 us -> 2690 us
    all_to_all x0 -> x1, blocking collectives: none -> 166 us  [face_read(): lax.all_to_all(jnp.stack(by_rank), group_axis, 0, 0)]
    all_gather x1 -> x0, waiting for transfers between devices: 134 us -> none  [join_rows(): return lax.all_gather(values, 'row', axis=0, tiled=True)]
  transfers between devices with their start and end apart: 16 -> 15, of which waited for: 15 -> 14; matrix products, arithmetic and copies ran while one was open for 3% -> 3% of each run, Pallas kernels for 0% -> 0%
where the time goes in v1:
time: 4370 us; the launch traced here: 4360 us
  waiting for transfers between devices  2690 us (62%)
  other arithmetic  776 us (18%)
  matrix products  413 us (9%)
  blocking collectives  278 us (6%)
  local copies, waits for them, and re-layouts  187 us (4%)
    psum x1, waiting for transfers between devices, on_device(): lax.psum(project(ffn_all, up_weight).astype(jnp.bfloat16), 'row')  1000 us
    reduce_scatter x1, waiting for transfers between devices, split_rows(): lax.psum_scatter(first, 'row', scatter_dimension=0, tiled=True)  719 us
    another operation x56, other arithmetic, block_step(): jax.scipy.linalg.solve_triangular(system, target, lower=True, unit_diagon...  573 us
    all_gather x1, waiting for transfers between devices, join_grads(): lax.all_gather(first, 'row', axis=0, tiled=True)  356 us
    psum x1, waiting for transfers between devices, on_device(): lax.psum(mix_grad.astype(jnp.bfloat16), 'dp').astype(jnp.float32)  272 us
    all_to_all x1, blocking collectives, face_read(): lax.all_to_all(jnp.stack(by_rank), group_axis, 0, 0)  166 us
    reduce_scatter x1, waiting for transfers between devices, grads_to_rows(): lax.psum_scatter(term(jnp.int32(0), lax.axis_size('row') * out_rows).asty...  128 us
  transfers between devices with their start and end apart: 15, of which 14 were waited for; matrix products, arithmetic and copies ran while one was open for 3% of the time, Pallas kernels for 0%

profile of v1, /device:TPU:0, one launch (start us, length us, event | category | flops | bytes accessed | tf_op | source)
XLA Modules:
  0.0 4360.7 jit_solution(11294304532631077148)
XLA Ops:
  25.4 28.5 all-gather.7.cloned.1.call-done
  56.9 22.5 fusion.207
  84.8 718.6 %reduce-scatter.10.cloned.1.call-done = f32[448,6144]{1,0:T(8,128)} async-done(((f32[1792,6144]{1,0:T(8,128)}), f32[448,6144]{1,0:T(8,128)}) %reduce-scatter.10.cloned.1.call-update) | async-done | bytes 11010064 | tf_op jit(solution)/shard_map/reduce_scatter | solution.py:142
  874.3 405.6 %while.44 = (s32[]{:T(128)}, f32[1,8,128,256]{3,2,1,0:T(8,128)}, f32[7,1,8,64,256]{4,2,3,0,1:T(8,128)}, f32[7,1,8,128,256]{4,3,2,1,0:T(8,128)}, f32[7,1,8,64]{3,...) while((s32[]{:T(128)}, f32[1,8,128,256]{3,2,1,0:T(8,128)}, ...), condition=%wide.region_9.11_spmd.clone.clone, body=%wide.region_6.10_spmd.clone.clone.sunk | while | flops 908922432 | bytes 18620180 | solution.py:96
  877.6 40.0 custom-call.26
  933.9 40.0 custom-call.26
  992.0 40.0 custom-call.26
  1050.2 40.0 custom-call.26
  1108.3 40.0 custom-call.26
  1166.5 40.0 custom-call.26
  1224.7 40.0 custom-call.26
  1288.2 165.8 %all_to_all.5 = bf16[4,448,2048]{2,1,0:T(8,128)(2,1)S(1)} all-to-all(bf16[4,448,2048]{2,1,0:T(8,128)(2,1)S(1)} %stack.2), channel_id=1, replica_groups=mesh['dp'=4,'row'=4,'col'=2] {'row'}, dimensions={0} | all-to-all | bytes 14680064 | tf_op jit(solution)/shard_map/all_to_all | solution.py:15
  1462.6 28.0 reduce-scatter.12.cloned.1.call-done
  1532.2 22.2 all-gather.9.cloned.1.call-done
  1572.4 1000.2 %all-reduce.31.cloned.1.call-done = (bf16[1792,2816]{1,0:T(8,128)(2,1)}, bf16[1792,2816]{1,0:T(8,128)(2,1)}, bf16[1792,2816]{1,0:T(8,128)(2,1)}) async-done(((bf16[1792,2816]{1,0:T(8,128)(2,1)}, bf16[1792,2816]{1,0:T(8,128)(2,1)}, bf16[1792,2816]{1,0:T(8,128)(2,1)}), (bf16[1792,2816]{1,0:T(8,128)(2,1)}, bf16[1792,2816]{1,0:T(8,128)(2,1)}, bf16[1792,2816]{1,0:T(8,128)(2,1)})) %all-reduce.31.cloned.1.call-update) | async-done | bytes 30277648 | tf_op jit(solution)/shard_map/psum | solution.py:252
  2608.5 27.9 reduce-scatter.16.cloned.1.call-done
  2654.0 27.1 all-gather.13.cloned.1.call-done
  2690.3 127.8 %reduce-scatter.18.cloned.1.call-done = bf16[448,2048]{1,0:T(8,128)(2,1)} async-done(((bf16[1792,2048]{1,0:T(8,128)(2,1)}), bf16[448,2048]{1,0:T(8,128)(2,1)}) %reduce-scatter.18.cloned.1.call-update) | async-done | bytes 1835024 | tf_op jit(solution)/shard_map/reduce_scatter | solution.py:190
  2840.4 547.9 %while.43 = (s32[]{:T(128)}, f32[1,8,128,256]{2,3,1,0:T(8,128)}, f32[7,1,8,64,128]{4,2,3,0,1:T(8,128)}, f32[7,1,8,64,128]{4,2,3,0,1:T(8,128)}, f32[7,1,8,64,256]...) while((s32[]{:T(128)}, f32[1,8,128,256]{2,3,1,0:T(8,128)}, ...), condition=%wide.region_35.37_spmd.clone, body=%wide.region_23.36_spmd.clone.sunk | while | flops 2448786944 | bytes 53756548 | solution.py:96
  2851.0 40.7 custom-call.25
  2929.3 40.7 custom-call.25
  3007.7 40.7 custom-call.25
  3086.1 40.7 custom-call.25
  3164.4 40.7 custom-call.25
  3242.8 40.7 custom-call.25
  3321.2 40.7 custom-call.25
  3488.5 356.3 %all-gather.15.cloned.1.call-done = bf16[1792,6144]{1,0:T(8,128)(2,1)} async-done(((bf16[448,6144]{1,0:T(8,128)(2,1)}), bf16[1792,6144]{1,0:T(8,128)(2,1)}) %all-gather.15.cloned.1.call-update) | async-done | bytes 22020112 | tf_op jit(solution)/shard_map/all_gather | solution.py:153
  3844.9 19.4 add_convert_fusion.1
  3941.2 30.6 all-reduce.29.cloned.1.call-done
  3973.2 28.8 reduce-scatter.20.cloned.1.call-done
  4004.0 40.0 all-reduce.22
  4060.7 271.9 %all-reduce.33.cloned.1.call-done = (bf16[512,6144]{1,0:T(8,128)(2,1)}, bf16[2048,512]{1,0:T(8,128)(2,1)}, bf16[512,2816]{1,0:T(8,128)(2,1)}, bf16[512,2816]{1,0:T(8,128)(2,1)}, bf16[2816,512]{1,0:T(8,128)(2,1)}) async-done(((bf16[512,6144]{1,0:T(8,128)(2,1)}, bf16[2048,512]{1,0:T(8,128)(2,1)}, bf16[512,2816]{1,0:T(8,128)(2,1)}, bf16[512,2816]{1,0:T(8,128)(2,1)}, bf16[2816,512]{1,0:T(8,128)(2,1)}), ...) | async-done | bytes 17039376 | tf_op jit(solution)/shard_map/psum | solution.py:284
  (998 shorter events, 861.5 us)
Async XLA Ops:
  7.2 1557.4 %copy-start = (bf16[512,2816]{1,0:T(8,128)(2,1)S(1)}, bf16[512,2816]{1,0:T(8,128)(2,1)}, u32[]{:S(2)}) copy-start(bf16[512,2816]{1,0:T(8,128)(2,1)} %param.32) | copy-start | bytes 8650756
  7.2 46.6 %all-gather.7.cloned.1.call-start = ((), (), s32[]{:S(2)}) async-start(), calls=%async_computation.8 | async-start | bytes 2752512 | tf_op jit(solution)/shard_map/all_gather | solution.py:133
  25.3 56.9 %reduce-scatter.22.cloned.1.call-start = ((), (), s32[]{:S(2)}) async-start(), calls=%async_computation.20 | async-start | bytes 1146880
  56.9 746.5 %reduce-scatter.10.cloned.1.call-start = ((), (), s32[]{:S(2)}) async-start(), calls=%async_computation.9 | async-start | bytes 55050240 | tf_op jit(solution)/shard_map/reduce_scatter | solution.py:142
  79.5 1411.1 %reduce-scatter.12.cloned.1.call-start = ((), (), s32[]{:S(2)}) async-start(), calls=%async_computation.10 | async-start | bytes 2752512 | tf_op jit(solution)/shard_map/reduce_scatter | solution.py:163
  80.3 736.5 %copy-start.72 = (f32[8]{0:T(128)}, f32[8]{0:T(128)S(1)}, u32[]{:S(2)}) copy-start(f32[8]{0:T(128)S(1)} %exponential_negate_fusion) | copy-start | bytes 100
  80.4 752.4 %copy-start.58 = (f32[1,448]{1,0:T(1,128)}, f32[1,448]{1,0:T(1,128)S(1)}, u32[]{:S(2)}) copy-start(f32[1,448]{1,0:T(1,128)S(1)} %get-tuple-element.925) | copy-start | bytes 5380
  80.4 752.4 %copy-start.60 = (f32[1,448]{1,0:T(1,128)}, f32[1,448]{1,0:T(1,128)S(1)}, u32[]{:S(2)}) copy-start(f32[1,448]{1,0:T(1,128)S(1)} %get-tuple-element.926) | copy-start | bytes 5380
  80.4 752.4 %copy-start.62 = (f32[1,448]{1,0:T(1,128)}, f32[1,448]{1,0:T(1,128)S(1)}, u32[]{:S(2)}) copy-start(f32[1,448]{1,0:T(1,128)S(1)} %get-tuple-element.927) | copy-start | bytes 5380
  80.5 752.3 %copy-start.32 = (f32[1,4096]{1,0:T(1,128)}, f32[1,4096]{1,0:T(1,128)S(1)}, u32[]{:S(2)}) copy-start(f32[1,4096]{1,0:T(1,128)S(1)} %get-tuple-element.917) | copy-start | bytes 49156
  80.5 752.3 %copy-start.34 = (f32[1,4096]{1,0:T(1,128)}, f32[1,4096]{1,0:T(1,128)S(1)}, u32[]{:S(2)}) copy-start(f32[1,4096]{1,0:T(1,128)S(1)} %get-tuple-element.918) | copy-start | bytes 49156
  80.5 752.3 %copy-start.36 = (f32[1,4096]{1,0:T(1,128)}, f32[1,4096]{1,0:T(1,128)S(1)}, u32[]{:S(2)}) copy-start(f32[1,4096]{1,0:T(1,128)S(1)} %get-tuple-element.919) | copy-start | bytes 49156
  80.5 752.3 %copy-start.38 = (f32[1,4096]{1,0:T(1,128)}, f32[1,4096]{1,0:T(1,128)S(1)}, u32[]{:S(2)}) copy-start(f32[1,4096]{1,0:T(1,128)S(1)} %get-tuple-element.920) | copy-start | bytes 49156
  83.3 733.5 %copy-start.40 = (f32[1,448,8,1]{1,3,2,0:T(1,128)}, f32[1,448,8,1]{1,3,2,0:T(1,128)S(1)}, u32[]{:S(2)}) copy-start(f32[1,448,8,1]{1,3,2,0:T(1,128)S(1)} %get-tuple-element.921) | copy-start | bytes 43012
  83.9 732.9 %copy-start.30 = (f32[1,7,64,8]{2,1,3,0:T(8,128)}, f32[1,7,64,8]{2,1,3,0:T(8,128)S(1)}, u32[]{:S(2)}) copy-start(f32[1,7,64,8]{2,1,3,0:T(8,128)S(1)} %squeeze.150) | copy-start | bytes 43012
  1288.1 168.7 %copy-start.76 = (bf16[2048,512]{1,0:T(8,128)(2,1)S(1)}, bf16[2048,512]{1,0:T(8,128)(2,1)}, u32[]{:S(2)}) copy-start(bf16[2048,512]{1,0:T(8,128)(2,1)} %param.30) | copy-start | bytes 6291460
  1461.9 60.2 %all-gather.11.cloned.1.call-start = ((), (), s32[]{:S(2)}) async-start(), calls=%async_computation.13 | async-start | bytes 2752512 | tf_op jit(solution)/shard_map/all_gather | solution.py:137
  1462.5 91.8 %all-gather.9.cloned.1.call-start = ((), (), s32[]{:S(2)}) async-start(), calls=%async_computation.11 | async-start | bytes 2752512 | tf_op jit(solution)/shard_map/all_gather | solution.py:133
  1504.1 1146.6 %copy-start.49 = (f32[896]{0:T(1024)}, f32[896]{0:T(1024)S(1)}, u32[]{:S(2)}) copy-start(f32[896]{0:T(1024)S(1)} %add_rsqrt_fusion.2) | copy-start | bytes 10756
  1506.9 1065.7 %all-reduce.31.cloned.1.call-start = ((), (), s32[]{:S(2)}) async-start(), calls=%async_computation.21 | async-start | bytes 60555264 | tf_op jit(solution)/shard_map/psum | solution.py:252
  1572.4 1064.0 %reduce-scatter.16.cloned.1.call-start = ((), (), s32[]{:S(2)}) async-start(), calls=%async_computation.14 | async-start | bytes 2752512 | tf_op jit(solution)/shard_map/reduce_scatter | solution.py:177
  2608.4 72.6 %all-gather.13.cloned.1.call-start = ((), (), s32[]{:S(2)}) async-start(), calls=%async_computation.15 | async-start | bytes 2752512 | tf_op jit(solution)/shard_map/all_gather | solution.py:137
  2653.5 164.6 %reduce-scatter.18.cloned.1.call-start = ((), (), s32[]{:S(2)}) async-start(), calls=%async_computation.16 | async-start | bytes 9175040 | tf_op jit(solution)/shard_map/reduce_scatter | solution.py:190
  2690.3 1154.6 %all-gather.15.cloned.1.call-start = ((), (), s32[]{:S(2)}) async-start(), calls=%async_computation.17 | async-start | bytes 27525120 | tf_op jit(solution)/shard_map/all_gather | solution.py:153
  3470.2 501.5 %all-reduce.29.cloned.1.call-start = ((), (), s32[]{:S(2)}) async-start(), calls=%async_computation.19 | async-start | bytes 262144 | tf_op jit(solution)/shard_map/psum | solution.py:295
  3488.5 513.5 %reduce-scatter.20.cloned.1.call-start = ((), (), s32[]{:S(2)}) async-start(), calls=%async_computation.18 | async-start | bytes 2752512 | tf_op jit(solution)/shard_map/reduce_scatter | solution.py:177
  3864.3 192.6 %reduce-scatter.14.cloned.1.call-start = ((), (), s32[]{:S(2)}) async-start(), calls=%async_computation.12 | async-start | bytes 2752512 | tf_op jit(solution)/shard_map/reduce_scatter | solution.py:163
  3874.2 458.4 %all-reduce.33.cloned.1.call-start = ((), (), s32[]{:S(2)}) async-start(), calls=%async_computation.22 | async-start | bytes 34078720 | tf_op jit(solution)/shard_map/psum | solution.py:284
  3927.0 129.9 %copy-start.14 = (bf16[896,512]{1,0:T(8,128)(2,1)S(1)}, bf16[896,512]{1,0:T(8,128)(2,1)}, u32[]{:S(2)}) copy-start(bf16[896,512]{1,0:T(8,128)(2,1)} %reduce-scatter.12.cloned.1.call-done) | copy-start | bytes 2752516
  3927.0 129.9 %copy-start.21 = (bf16[896,512]{1,0:T(8,128)(2,1)S(1)}, bf16[896,512]{1,0:T(8,128)(2,1)}, u32[]{:S(2)}) copy-start(bf16[896,512]{1,0:T(8,128)(2,1)} %param.35) | copy-start | bytes 2752516
  3927.0 129.9 %copy-start.50 = (f32[896]{0:T(1024)S(1)}, f32[896]{0:T(1024)}, u32[]{:S(2)}) copy-start(f32[896]{0:T(1024)} %copy-done.49) | copy-start | bytes 10756
  3927.0 129.9 %copy-start.57 = (f32[896]{0:T(1024)S(1)}, f32[896]{0:T(1024)}, u32[]{:S(2)}) copy-start(f32[896]{0:T(1024)} %copy-done.56) | copy-start | bytes 10756
  (113 other events, 1988.0 us)
Sparse Core Ops, SparseCore 0:
  25.4 28.3 all-gather.6
  57.0 25.0 reduce-scatter.21
  84.5 718.8 reduce-scatter.9
  1462.1 28.4 reduce-scatter.11
  1492.0 30.1 all-gather.10
  1524.2 30.1 all-gather.8
  1572.5 1000.0 all-reduce.30
  2608.6 27.7 reduce-scatter.15
  2653.6 27.3 all-gather.12
  2690.4 127.7 reduce-scatter.17
  3470.3 374.4 all-gather.14
  3850.8 120.8 all-reduce.28
  3974.0 27.9 reduce-scatter.19
  4004.2 29.4 reduce-scatter.13
  4037.7 294.8 all-reduce.32
